TPU v7x, 512 devices: a whole 4x4x16 slice. The times are simulated.
512 devices in a mesh: dp: 64 (over y_lo, z, core), blk: 8 (over y_hi, x).
Axes of the slice: x: 4, y: 4 (y_hi: 2, y_lo: 2; y = y_hi * 2 + y_lo), z: 16, core: 2. Of those that a mesh axis runs over, the one named last changes fastest.
Arguments:
- resid: bfloat16 [2048, 2048], P('dp'), may hold values from -40 to 40
- queries: bfloat16 [2048, 16, 128], P('dp', 'blk'), may hold values from -60 to 60
- new_kv: bfloat16 [2048, 2, 8, 128], P('dp', None, 'blk'), may hold values from -6 to 6
- prefix_pool: bfloat16 [2048, 128, 2, 8, 128], P('dp', None, None, 'blk'), may hold values from -6 to 6
- page_table: int32 [64, 32], P('dp'), may hold values from 0 to 31, each once within a row
- prompt_len: int32 [64], P('dp'), may hold values from 1 to 4096, 131072 in all
- tail_pool: bfloat16 [1024, 128, 2, 8, 128], P('dp', None, None, 'blk'), may hold values from -6 to 6
- tail_len: int32 [64, 16], P('dp'), may hold values from 1 to 128, 1024 in all within a row
- migration: int32 [1024], replicated, may hold values from 0 to 1023, each once
- out_w: bfloat16 [2048, 2048], P('blk'), may hold values from -0.125 to 0.125
- mlp_gain: bfloat16 [2048], replicated, may hold values from 0.099609375 to 1.8984375
- gate_w: bfloat16 [2048, 6144], P('blk', 'dp'), may hold values from -0.125 to 0.125
- up_w: bfloat16 [2048, 6144], P('blk', 'dp'), may hold values from -0.125 to 0.125
- down_w: bfloat16 [6144, 2048], P('dp', 'blk'), may hold values from -0.078125 to 0.078125
- final_gain: bfloat16 [2048], P('blk'), may hold values from 0.099609375 to 1.8984375
- score_w: bfloat16 [2048], P('blk'), may hold values from -0.125 to 0.125
Outputs:
- hidden_out: bfloat16 [2048, 2048], P('dp', 'blk')
- score: float32 [2048], P('dp')
Inputs may be any that keep to these rules, and one draw needn't show every extreme that they name: `page_table`: each row lists every page of the device's pool once. `migration`: names every continuation once.
All inputs are finite; a program needn't handle non-finite values. No bound on the sum of `prompt_len` on one device may be relied on, other than what follows from the above.
Results may differ from a plain program's by a relative error of at most 0.012.
Values may be sent and summed in bfloat16 or wider, within the bound.
A program may use at most 64 MiB of HBM per device.

v0:
```python
import math
import jax
import jax.numpy as jnp
from jax import lax
from jax.sharding import PartitionSpec as P

D = 2048
NEW = 2
NEG = -1e30
EPS = 1e-06


def attend_prompt(queries, pool, table, prompt_len, tails, tail_len, pairs):
    token_rows, heads, width = queries.shape
    groups = pairs.shape[2]
    repeat = heads // groups
    conts = tails.shape[0]
    fresh = token_rows // conts
    prefix = jnp.take(pool, table, axis=0).reshape(-1, 2, groups, width)
    span = prefix.shape[0]
    grouped = queries.reshape(conts, fresh, groups, repeat, width)
    recent = pairs.reshape(conts, fresh, 2, groups, width)
    factor = 1.0 / math.sqrt(width)
    pre_scores = (
        jnp.einsum("cngrd,pgd->gcnrp", grouped, prefix[:, 0], preferred_element_type=jnp.float32)
        * factor
    )
    tail_scores = (
        jnp.einsum("cngrd,ctgd->gcnrt", grouped, tails[:, :, 0], preferred_element_type=jnp.float32)
        * factor
    )
    new_scores = (
        jnp.einsum(
            "cngrd,cmgd->gcnrm", grouped, recent[:, :, 0], preferred_element_type=jnp.float32
        )
        * factor
    )
    pre_mask = (jnp.arange(span) < prompt_len)[None, None, None, None, :]
    tail_mask = (jnp.arange(tails.shape[1])[None, :] < tail_len[:, None])[None, :, None, None, :]
    new_mask = (jnp.arange(fresh)[None, :] <= jnp.arange(fresh)[:, None])[None, None, :, None, :]
    pre_scores = jnp.where(pre_mask, pre_scores, NEG)
    tail_scores = jnp.where(tail_mask, tail_scores, NEG)
    new_scores = jnp.where(new_mask, new_scores, NEG)
    highest = jnp.maximum(
        jnp.maximum(jnp.max(pre_scores, -1), jnp.max(tail_scores, -1)), jnp.max(new_scores, -1)
    )[..., None]
    pre_weights = jnp.where(pre_mask, jnp.exp(pre_scores - highest), 0.0)
    tail_weights = jnp.where(tail_mask, jnp.exp(tail_scores - highest), 0.0)
    new_weights = jnp.where(new_mask, jnp.exp(new_scores - highest), 0.0)
    total = jnp.sum(pre_weights, -1) + jnp.sum(tail_weights, -1) + jnp.sum(new_weights, -1)
    mixed = jnp.einsum(
        "gcnrp,pgd->cngrd",
        pre_weights.astype(jnp.bfloat16),
        prefix[:, 1],
        preferred_element_type=jnp.float32,
    )
    mixed = mixed + jnp.einsum(
        "gcnrt,ctgd->cngrd",
        tail_weights.astype(jnp.bfloat16),
        tails[:, :, 1],
        preferred_element_type=jnp.float32,
    )
    mixed = mixed + jnp.einsum(
        "gcnrm,cmgd->cngrd",
        new_weights.astype(jnp.bfloat16),
        recent[:, :, 1],
        preferred_element_type=jnp.float32,
    )
    mixed = mixed / jnp.transpose(total, (1, 2, 0, 3))[..., None]
    return mixed.reshape(token_rows, heads * width).astype(jnp.bfloat16)


def shards(
    resid,
    queries,
    new_kv,
    prefix_pool,
    page_table,
    prompt_len,
    tail_pool,
    tail_len,
    migration,
    out_w,
    mlp_gain,
    gate_w,
    up_w,
    down_w,
    final_gain,
    score_w,
):
    token_rows = resid.shape[0]
    attn = attend_prompt(
        queries, prefix_pool, page_table[0], prompt_len[0], tail_pool, tail_len[0], new_kv
    )
    partial_value = jnp.dot(attn, out_w, preferred_element_type=jnp.float32)
    mixed = lax.psum(partial_value.astype(jnp.bfloat16), "blk").astype(jnp.float32)
    middle = resid.astype(jnp.float32) + mixed
    normed = (
        middle
        * lax.rsqrt(jnp.mean(middle * middle, -1, keepdims=True) + EPS)
        * mlp_gain.astype(jnp.float32)
    ).astype(jnp.bfloat16)
    feat_width = gate_w.shape[0]
    units = gate_w.shape[1]
    block_index = lax.axis_index("blk")
    home_index = lax.axis_index("dp")
    feat_slice = lax.dynamic_slice_in_dim(normed, block_index * feat_width, feat_width, 1)
    middle_slice = lax.dynamic_slice_in_dim(middle, block_index * feat_width, feat_width, 1)
    piece = lax.all_gather(feat_slice, "dp", axis=0, tiled=True)
    partial_units = jnp.concatenate(
        [
            jnp.dot(piece, gate_w, preferred_element_type=jnp.float32),
            jnp.dot(piece, up_w, preferred_element_type=jnp.float32),
        ],
        axis=1,
    )
    summed = lax.psum(partial_units.astype(jnp.bfloat16), "blk").astype(jnp.float32)
    hidden = (jax.nn.silu(summed[:, :units]) * summed[:, units:]).astype(jnp.bfloat16)
    source = (migration[:, None] * NEW + jnp.arange(NEW, dtype=jnp.int32)[None, :]).reshape(-1)
    term = jnp.dot(jnp.take(hidden, source, axis=0), down_w, preferred_element_type=jnp.float32)
    local_rows = source - home_index * token_rows
    own_rows = (local_rows >= 0) & (local_rows < token_rows)
    carried = jnp.take(middle_slice, jnp.clip(local_rows, 0, token_rows - 1), axis=0)
    moved = lax.psum_scatter(
        term + jnp.where(own_rows[:, None], carried, 0.0), "dp", scatter_dimension=0, tiled=True
    )
    weighted = final_gain.astype(jnp.float32) * score_w.astype(jnp.float32)
    squares, terms = lax.psum((jnp.sum(moved * moved, -1), jnp.sum(moved * weighted, -1)), "blk")
    score = terms * lax.rsqrt(squares / D + EPS)
    return (moved.astype(jnp.bfloat16), score)


def solution(mesh):
    return jax.shard_map(
        shards,
        mesh=mesh,
        in_specs=(
            P("dp", None),
            P("dp", "blk", None),
            P("dp", None, "blk", None),
            P("dp", None, None, "blk", None),
            P("dp", None),
            P("dp"),
            P("dp", None, None, "blk", None),
            P("dp", None),
            P(),
            P("blk", None),
            P(),
            P("blk", "dp"),
            P("blk", "dp"),
            P("dp", "blk"),
            P("blk"),
            P("blk"),
        ),
        out_specs=(P("dp", "blk"), P("dp")),
        check_vma=False,
    )
```

profile of v0, /device:TPU:8, one launch (start us, length us, event | category | flops | bytes accessed | tf_op | source)
XLA Modules:
  0.0 631.7 jit_solution(11279439814743314583)
XLA Ops:
  7.2 0.8 fusion.25
  8.0 0.7 compare_and_fusion.3
  9.4 6.2 gather_fusion
  15.5 3.6 copy.69
  19.1 0.1 broadcast_bitcast_fusion
  19.3 2.3 fusion.31
  21.6 0.5 fusion.33
  22.1 0.1 copy.72
  22.2 0.4 fusion.22
  22.6 0.1 copy.74
  22.7 2.0 broadcast_select_fusion
  24.7 1.3 copy-done.2
  26.0 0.6 fusion.32
  26.6 0.1 fusion.24
  26.7 0.1 copy.77
  26.8 0.1 fusion.30
  26.9 0.2 fusion.26
  27.1 0.1 copy.82
  27.2 0.4 copy-done.4
  27.6 0.3 fusion.7
  27.9 1.6 fusion.11
  29.5 0.1 copy.80
  29.7 0.2 fusion.23
  29.8 2.0 fusion.6
  31.9 0.9 convolution_convert_fusion.2
  32.9 0.8 dynamic-slice
  33.6 102.1 %all-reduce.4.cloned.1.call-done = bf16[32,2048]{1,0:T(8,128)(2,1)} async-done(((bf16[32,2048]{1,0:T(8,128)(2,1)}), bf16[32,2048]{1,0:T(8,128)(2,1)}) %all-reduce.4.cloned.1.call-update) | async-done | bytes 131088 | tf_op jit(solution)/shard_map/psum | solution.py:96
  135.7 1.1 convert_add_fusion
  136.8 0.7 multiply_convert_fusion
  137.6 0.2 iota_add_fusion
  137.8 0.3 add.179
  138.1 0.3 add.163
  138.4 119.5 %all-gather.2.cloned.1.call-done = bf16[2048,256]{1,0:T(8,128)(2,1)} async-done(((bf16[32,256]{1,0:T(8,128)(2,1)}), bf16[2048,256]{1,0:T(8,128)(2,1)}) %all-gather.2.cloned.1.call-update) | async-done | bytes 1048592 | tf_op jit(solution)/shard_map/all_gather | solution.py:109
  257.9 1.7 convolution_convert_fusion
  259.6 1.7 convolution_convert_fusion.1
  261.3 0.9 pad_maximum_fusion
  262.4 8.6 %gather_fusion.2 = f32[2048,256]{1,0:T(8,128)} fusion(f32[32,256]{1,0:T(8,128)S(1)} %get-tuple-element.7, s32[2048]{0:T(1024)S(1)} %broadcast_clamp_fusion), kind=kCustom, calls=%fused_computation.2 | custom fusion | bytes 4202496 | tf_op jit(solution)/shard_map/jit(_take)/gather | solution.py:123
  270.9 89.1 %all-reduce.6.cloned.1.call-done = bf16[2048,192]{0,1:T(8,128)(2,1)} async-done(((bf16[2048,192]{0,1:T(8,128)(2,1)}), bf16[2048,192]{0,1:T(8,128)(2,1)}) %all-reduce.6.cloned.1.call-update) | async-done | bytes 786448 | tf_op jit(solution)/shard_map/psum | solution.py:117
  360.0 1.3 convert_element_type.59
  361.3 0.2 fusion.9
  361.6 0.3 copy.86
  361.9 6.2 gather_fusion.1
  368.1 4.9 convolution_add_fusion
  372.9 0.6 copy-done.12
  373.6 226.0 %reduce-scatter.2.cloned.1.call-done = f32[32,256]{1,0:T(8,128)} async-done(((f32[2048,256]{1,0:T(8,128)}), f32[32,256]{1,0:T(8,128)}) %reduce-scatter.2.cloned.1.call-update) | async-done | bytes 32784 | tf_op jit(solution)/shard_map/reduce_scatter | solution.py:124
  599.6 1.5 multiply_reduce_fusion.1
  601.1 23.5 %all-reduce = (f32[32]{0:T(128)S(1)}, f32[32]{0:T(128)S(1)}) all-reduce(f32[32]{0:T(128)S(1)} %get-tuple-element.3, f32[32]{0:T(128)S(1)} %get-tuple-element.2), channel_id=1, replica_groups=mesh['dp'=64,'blk'=8] {'blk'}, use_global_device_ids=true, to_apply=%region_11.12 | all-reduce | flops 64 | bytes 512 | tf_op jit(solution)/shard_map/psum | solution.py:128
  624.6 0.5 rsqrt_multiply_fusion
  (50 shorter events, 0.5 us)
Async XLA Ops:
  7.2 2.2 copy-start
  7.2 128.6 %all-reduce.4.cloned.1.call-start = ((), (), s32[]{:S(2)}) async-start(), calls=%async_computation.1 | async-start | bytes 262144 | tf_op jit(solution)/shard_map/psum | solution.py:96
  15.5 3.7 copy-start.11
  15.5 3.7 copy-start.1
  19.3 2.3 copy-start.14
  19.3 2.9 copy-start.9
  24.7 1.4 copy-start.2
  26.6 1.0 copy-start.4
  27.9 3.9 copy-start.3
  29.8 105.9 %copy-start.5 = (bf16[32,2048]{1,0:T(8,128)(2,1)S(1)}, bf16[32,2048]{1,0:T(8,128)(2,1)}, u32[]{:S(2)}) copy-start(bf16[32,2048]{1,0:T(8,128)(2,1)} %param.16) | copy-start | bytes 393220
  29.8 107.7 %copy-start.10 = (s32[1024]{0:T(1024)S(1)}, s32[1024]{0:T(1024)}, u32[]{:S(2)}) copy-start(s32[1024]{0:T(1024)} %param.24) | copy-start | bytes 12292
  31.8 226.1 %copy-start.7 = (bf16[256,96]{0,1:T(8,128)(2,1)S(1)}, bf16[256,96]{0,1:T(8,128)(2,1)}, u32[]{:S(2)}) copy-start(bf16[256,96]{0,1:T(8,128)(2,1)} %param.28) | copy-start | bytes 147460
  32.8 226.8 %copy-start.8 = (bf16[256,96]{0,1:T(8,128)(2,1)S(1)}, bf16[256,96]{0,1:T(8,128)(2,1)}, u32[]{:S(2)}) copy-start(bf16[256,96]{0,1:T(8,128)(2,1)} %param.27) | copy-start | bytes 147460
  32.8 225.1 %all-gather.2.cloned.1.call-start = ((), (), s32[]{:S(2)}) async-start(), calls=%async_computation.2 | async-start | bytes 1064960 | tf_op jit(solution)/shard_map/all_gather | solution.py:109
  137.5 222.5 %all-reduce.6.cloned.1.call-start = ((), (), s32[]{:S(2)}) async-start(), calls=%async_computation.3 | async-start | bytes 1572864 | tf_op jit(solution)/shard_map/psum | solution.py:117
  262.2 337.3 %reduce-scatter.2.cloned.1.call-start = ((), (), s32[]{:S(2)}) async-start(), calls=%async_computation.4 | async-start | bytes 2129920 | tf_op jit(solution)/shard_map/reduce_scatter | solution.py:124
  361.8 6.2 copy-start.6
  372.9 0.7 copy-start.12
  372.9 0.7 copy-start.13
Sparse Core Ops, SparseCore 0:
  32.9 102.7 all-reduce.3
  138.7 119.1 all-gather.1
  262.4 97.6 all-reduce.5
  373.1 226.4 reduce-scatter.1
where the time goes:
time: 632 us
  waiting for transfers between devices  537 us (85%)
  local copies, waits for them, and re-layouts  31.4 us (5%)
  blocking collectives  23.5 us (4%)
  between operations  14.7 us (2%)
  matrix products  14.3 us (2%)
  other arithmetic  10.8 us (2%)
    reduce_scatter x1, waiting for transfers between devices, shards(): lax.psum_scatter(term + jnp.where(own_rows[:, None], carried, 0.0), 'dp',...  226 us
    all_gather x1, waiting for transfers between devices, shards(): piece = lax.all_gather(feat_slice, 'dp', axis=0, tiled=True)  120 us
    psum x1, waiting for transfers between devices, shards(): lax.psum(partial_value.astype(jnp.bfloat16), 'blk').astype(jnp.float32)  102 us
    psum x1, waiting for transfers between devices, shards(): lax.psum(partial_units.astype(jnp.bfloat16), 'blk').astype(jnp.float32)  89.1 us
    psum x1, blocking collectives, shards(): lax.psum((jnp.sum(moved * moved, -1), jnp.sum(moved * weighted, -1)), 'blk')  23.5 us
  transfers between devices with their start and end apart: 4, of which 4 were waited for; matrix products, arithmetic and copies ran while one was open for 2% of the time, Pallas kernels for 0%

commit v1 on v0

--- a/solution.py
+++ b/solution.py
@@ -106,7 +106,9 @@
     home_index = lax.axis_index("dp")
     feat_slice = lax.dynamic_slice_in_dim(normed, block_index * feat_width, feat_width, 1)
     middle_slice = lax.dynamic_slice_in_dim(middle, block_index * feat_width, feat_width, 1)
-    piece = lax.all_gather(feat_slice, "dp", axis=0, tiled=True)
+    piece = jnp.concatenate(
+        lax.all_to_all(jnp.stack([feat_slice] * lax.axis_size("dp")), "dp", 0, 0), axis=0
+    )
     partial_units = jnp.concatenate(
         [
             jnp.dot(piece, gate_w, preferred_element_type=jnp.float32),

time: 632 us -> 573 us (0.907)
  waiting for transfers between devices: 537 us -> 462 us
  starting transfers between devices: 0.16 us -> 14.6 us
    all_gather x1 -> x0, waiting for transfers between devices: 120 us -> none  [shards(): piece = lax.all_gather(feat_slice, 'dp', axis=0, tiled=True)]
    all_to_all x0 -> x1, waiting for transfers between devices: none -> 48.3 us  [shards(): lax.all_to_all(jnp.stack([feat_slice] * lax.axis_size('dp')), 'dp', 0, 0)]
    all_to_all x0 -> x1, starting transfers between devices: none -> 14.4 us  [shards(): lax.all_to_all(jnp.stack([feat_slice] * lax.axis_size('dp')), 'dp', 0, 0)]
where the time goes in v1:
time: 573 us; the launch traced here: 572 us
  waiting for transfers between devices  462 us (81%)
  local copies, waits for them, and re-layouts  34.6 us (6%)
  blocking collectives  23.5 us (4%)
  between operations  14.7 us (3%)
  starting transfers between devices  14.6 us (3%)
  matrix products  11.9 us (2%)
  other arithmetic  11 us (2%)
    reduce_scatter x1, waiting for transfers between devices, shards(): lax.psum_scatter(term + jnp.where(own_rows[:, None], carried, 0.0), 'dp',...  226 us
    psum x1, waiting for transfers between devices, shards(): lax.psum(partial_value.astype(jnp.bfloat16), 'blk').astype(jnp.float32)  102 us
    psum x1, waiting for transfers between devices, shards(): lax.psum(partial_units.astype(jnp.bfloat16), 'blk').astype(jnp.float32)  85.6 us
    all_to_all x1, waiting for transfers between devices, shards(): lax.all_to_all(jnp.stack([feat_slice] * lax.axis_size('dp')), 'dp', 0, 0)  48.3 us
    psum x1, blocking collectives, shards(): lax.psum((jnp.sum(moved * moved, -1), jnp.sum(moved * weighted, -1)), 'blk')  23.5 us
    all_to_all x1, starting transfers between devices, shards(): lax.all_to_all(jnp.stack([feat_slice] * lax.axis_size('dp')), 'dp', 0, 0)  14.4 us
  transfers between devices with their start and end apart: 4, of which 4 were waited for; matrix products, arithmetic and copies ran while one was open for 2% of the time, Pallas kernels for 0%

profile of v1, /device:TPU:8, one launch (start us, length us, event | category | flops | bytes accessed | tf_op | source)
XLA Modules:
  0.0 572.3 jit_solution(15055319768376023194)
XLA Ops:
  7.2 0.8 fusion.25
  8.0 0.7 compare_and_fusion.3
  9.4 6.2 %gather_fusion = bf16[32,128,2,128]{3,2,1,0:T(2,128)(2,1)} fusion(bf16[32,128,2,128]{3,2,1,0:T(2,128)(2,1)S(1)} %bitcast.105, s32[1024]{0:T(1024)S(1)} %pad_clamp_fusion), kind=kCustom, calls=%fused_computation | custom fusion | bytes 4194432 | tf_op jit(solution)/shard_map/jit(_take)/gather | solution.py:19
  15.5 3.6 copy.69
  19.3 2.3 fusion.31
  21.6 0.5 fusion.33
  22.1 0.1 copy.72
  22.2 0.4 fusion.22
  22.6 0.1 copy.74
  22.7 2.0 broadcast_select_fusion
  24.7 1.3 copy-done.2
  26.0 0.6 fusion.32
  26.6 0.1 fusion.24
  26.7 0.1 copy.77
  26.8 0.1 fusion.30
  26.9 0.2 fusion.26
  27.1 0.1 copy.82
  27.2 0.4 copy-done.4
  27.6 0.3 fusion.7
  27.9 1.6 fusion.11
  29.5 0.1 copy.80
  29.7 0.2 fusion.23
  29.8 1.9 fusion.6
  31.8 0.9 convolution_convert_fusion.2
  32.8 0.8 dynamic-slice
  33.6 102.2 %all-reduce.4.cloned.1.call-done = bf16[32,2048]{1,0:T(8,128)(2,1)} async-done(((bf16[32,2048]{1,0:T(8,128)(2,1)}), bf16[32,2048]{1,0:T(8,128)(2,1)}) %all-reduce.4.cloned.1.call-update) | async-done | bytes 131088 | tf_op jit(solution)/shard_map/psum | solution.py:96
  135.7 1.1 convert_add_fusion
  136.9 1.1 stack.2
  138.0 14.4 %all-to-all-start = ((bf16[64,32,256]{2,1,0:T(8,128)(2,1)}), bf16[64,32,256]{2,1,0:T(8,128)(2,1)S(1)}, u32[]{:S(2)}, u32[]{:S(2)}) async-start(bf16[64,32,256]{2,1,0:T(8,128)(2,1)} %stack.2), calls=%async_computation | async-start | bytes 2097152 | tf_op jit(solution)/shard_map/all_to_all | solution.py:110
  152.5 1.0 iota_add_fusion
  153.5 1.4 add.179
  154.9 1.3 add.163
  156.2 48.3 %all-to-all-done = bf16[64,32,256]{2,1,0:T(8,128)(2,1)S(1)} async-done(((bf16[64,32,256]{2,1,0:T(8,128)(2,1)}), bf16[64,32,256]{2,1,0:T(8,128)(2,1)S(1)}, u32[]{:S(2)}, u32[]{:S(2)}) %all-to-all-start) | async-done | bytes 1048608 | tf_op jit(solution)/shard_map/all_to_all | solution.py:110
  204.5 0.4 convolution_convert_fusion
  205.0 0.4 convolution_convert_fusion.1
  205.4 0.9 pad_maximum_fusion
  206.5 8.6 %gather_fusion.2 = f32[2048,256]{1,0:T(8,128)} fusion(f32[32,256]{1,0:T(8,128)S(1)} %get-tuple-element.7, s32[2048]{0:T(1024)S(1)} %broadcast_clamp_fusion), kind=kCustom, calls=%fused_computation.2 | custom fusion | bytes 4202496 | tf_op jit(solution)/shard_map/jit(_take)/gather | solution.py:125
  215.1 85.6 %all-reduce.6.cloned.1.call-done = bf16[2048,192]{0,1:T(8,128)(2,1)} async-done(((bf16[2048,192]{0,1:T(8,128)(2,1)}), bf16[2048,192]{0,1:T(8,128)(2,1)}) %all-reduce.6.cloned.1.call-update) | async-done | bytes 786448 | tf_op jit(solution)/shard_map/psum | solution.py:119
  300.7 1.3 convert_element_type.59
  302.0 0.2 fusion.9
  302.2 0.3 copy.86
  302.5 6.2 %gather_fusion.1 = bf16[2048,96]{1,0:T(8,128)(2,1)S(1)} fusion(bf16[2048,96]{1,0:T(8,128)(2,1)S(1)} %copy.86, s32[2048]{0:T(1024)S(1)} %broadcast_clamp_fusion.1), kind=kCustom, calls=%fused_computation.1 | custom fusion | bytes 794624 | tf_op jit(solution)/shard_map/jit(_take)/gather | solution.py:122
  308.7 4.9 convolution_add_fusion
  313.6 0.6 copy-done.12
  314.2 226.0 %reduce-scatter.2.cloned.1.call-done = f32[32,256]{1,0:T(8,128)} async-done(((f32[2048,256]{1,0:T(8,128)}), f32[32,256]{1,0:T(8,128)}) %reduce-scatter.2.cloned.1.call-update) | async-done | bytes 32784 | tf_op jit(solution)/shard_map/reduce_scatter | solution.py:126
  540.2 1.5 multiply_reduce_fusion.1
  541.8 23.5 %all-reduce = (f32[32]{0:T(128)S(1)}, f32[32]{0:T(128)S(1)}) all-reduce(f32[32]{0:T(128)S(1)} %get-tuple-element.3, f32[32]{0:T(128)S(1)} %get-tuple-element.2), channel_id=1, replica_groups=mesh['dp'=64,'blk'=8] {'blk'}, use_global_device_ids=true, to_apply=%region_11.12 | all-reduce | flops 64 | bytes 512 | tf_op jit(solution)/shard_map/psum | solution.py:130
  565.3 0.5 rsqrt_multiply_fusion
  (50 shorter events, 0.6 us)
Async XLA Ops:
  7.2 2.2 copy-start
  7.2 128.5 %all-reduce.4.cloned.1.call-start = ((), (), s32[]{:S(2)}) async-start(), calls=%async_computation.2 | async-start | bytes 262144 | tf_op jit(solution)/shard_map/psum | solution.py:96
  15.5 3.7 copy-start.11
  15.5 3.7 copy-start.1
  19.3 2.3 copy-start.14
  19.3 2.9 copy-start.9
  24.7 1.4 copy-start.2
  26.6 1.0 copy-start.4
  27.9 3.9 copy-start.3
  29.8 105.9 %copy-start.5 = (bf16[32,2048]{1,0:T(8,128)(2,1)S(1)}, bf16[32,2048]{1,0:T(8,128)(2,1)}, u32[]{:S(2)}) copy-start(bf16[32,2048]{1,0:T(8,128)(2,1)} %param.16) | copy-start | bytes 393220
  32.8 119.7 %copy-start.10 = (s32[1024]{0:T(1024)S(1)}, s32[1024]{0:T(1024)}, u32[]{:S(2)}) copy-start(s32[1024]{0:T(1024)} %param.24) | copy-start | bytes 12292
  138.0 66.5 %copy-start.7 = (bf16[256,96]{0,1:T(8,128)(2,1)S(1)}, bf16[256,96]{0,1:T(8,128)(2,1)}, u32[]{:S(2)}) copy-start(bf16[256,96]{0,1:T(8,128)(2,1)} %param.28) | copy-start | bytes 147460
  138.0 67.0 %copy-start.8 = (bf16[256,96]{0,1:T(8,128)(2,1)S(1)}, bf16[256,96]{0,1:T(8,128)(2,1)}, u32[]{:S(2)}) copy-start(bf16[256,96]{0,1:T(8,128)(2,1)} %param.27) | copy-start | bytes 147460
  138.0 66.5 %all-to-all-start = ((bf16[64,32,256]{2,1,0:T(8,128)(2,1)}), bf16[64,32,256]{2,1,0:T(8,128)(2,1)S(1)}, u32[]{:S(2)}, u32[]{:S(2)}) async-start(bf16[64,32,256]{2,1,0:T(8,128)(2,1)} %stack.2), calls=%async_computation | async-start | bytes 2097152 | tf_op jit(solution)/shard_map/all_to_all | solution.py:110
  152.4 148.2 %all-reduce.6.cloned.1.call-start = ((), (), s32[]{:S(2)}) async-start(), calls=%async_computation.3 | async-start | bytes 1572864 | tf_op jit(solution)/shard_map/psum | solution.py:119
  206.4 333.9 %reduce-scatter.2.cloned.1.call-start = ((), (), s32[]{:S(2)}) async-start(), calls=%async_computation.4 | async-start | bytes 2129920 | tf_op jit(solution)/shard_map/reduce_scatter | solution.py:126
  302.5 6.2 %copy-start.6 = (bf16[96,256]{1,0:T(8,128)(2,1)S(1)}, bf16[96,256]{1,0:T(8,128)(2,1)}, u32[]{:S(2)}) copy-start(bf16[96,256]{1,0:T(8,128)(2,1)} %param.29) | copy-start | bytes 147460
  313.6 0.7 copy-start.12
  313.6 0.7 copy-start.13
Sparse Core Ops, SparseCore 0:
  32.9 102.7 all-reduce.3
  206.5 94.1 all-reduce.5
  313.7 226.4 reduce-scatter.1
